TPU v7x, 512 devices: a whole 4x8x8 slice. The times are simulated.
512 devices in a mesh: gossip: 16 (over z, y_lo), shard: 32 (over x, y_hi, core).
Axes of the slice: x: 4, y: 8 (y_hi: 4, y_lo: 2; y = y_hi * 2 + y_lo), z: 8, core: 2. Of those that a mesh axis runs over, the one named last changes fastest.
Arguments:
- inputs: bfloat16 [16, 13824, 2020], P('gossip', 'shard'), may hold values from -6 to 6
- upstream: bfloat16 [16, 13824, 1010], P('gossip', 'shard'), may hold values from -6 to 6
- params: float32 [16, 2048, 1010], P('gossip', 'shard'), may hold values from -0.125 to 0.125
- ps_weight: float32 [16], P('gossip'), may hold values from 0.5 to 2
- step: int32 [1], replicated, may hold values from 0 to 999
- cycle_order: int32 [16], replicated, may hold values from 0 to 15, each once
Outputs:
- grad_in: bfloat16 [16, 13824, 2020], P('gossip', 'shard')
- new_params: float32 [16, 2048, 1010], P('gossip', 'shard')
- new_weight: float32 [16], P('gossip')
Inputs may be any that keep to these rules, and one draw needn't show every extreme that they name: cycle_order names every group once.
All inputs are finite; a program needn't handle non-finite values.
Results may differ from a plain program's by a relative error of at most 0.0061.
Values may be sent and summed in bfloat16 or wider, within the bound.
No kernel may reach another device: no remote copies, remote signals or barrier semaphores. Data moves between devices by JAX's collectives and lax.ppermute only.
A program may use at most 64 MiB of HBM per device.

v0:
```python
import jax
import jax.numpy as jnp
from jax import lax
from jax.sharding import PartitionSpec as P

learn_rate = 0.5


def body(inputs, upstream, params, ps_weight, step, cycle_order):
    x_rows = inputs[0]
    up_rows = upstream[0]
    own_shard = params[0]
    weight = ps_weight[0]
    shard_rows = own_shard.shape[0]
    n_shard = lax.axis_size("shard")
    padded_width = shard_rows * n_shard
    in_width = x_rows.shape[1]
    x_padded = jnp.pad(x_rows, ((0, 0), (0, padded_width - in_width)))
    debiased = (own_shard / weight).astype(jnp.bfloat16)
    contract_cols = (((1,), (1,)), ((), ()))
    gathered = lax.all_gather(debiased, "shard", axis=0, tiled=True)
    pre_act = jnp.dot(x_padded, gathered, preferred_element_type=jnp.float32)
    sigmoid_pre = jax.nn.sigmoid(pre_act)
    d_pre = (
        up_rows.astype(jnp.float32) * sigmoid_pre * (1.0 + pre_act * (1.0 - sigmoid_pre))
    ).astype(jnp.bfloat16)
    back_full = lax.dot_general(d_pre, gathered, contract_cols, preferred_element_type=jnp.float32)
    grad_in = back_full[:, :in_width].astype(jnp.bfloat16)
    contract_rows = (((0,), (0,)), ((), ()))
    local_grad = lax.dot_general(x_padded, d_pre, contract_rows, preferred_element_type=jnp.float32)
    summed = lax.psum(local_grad.astype(jnp.bfloat16), "shard").astype(jnp.float32)
    my_rows = lax.dynamic_slice_in_dim(summed, lax.axis_index("shard") * shard_rows, shard_rows, 0)
    group_tokens = x_rows.shape[0] * n_shard
    stepped = own_shard - learn_rate * my_rows / group_tokens
    n_groups = lax.axis_size("gossip")
    levels = n_groups.bit_length() - 1
    distance = jnp.left_shift(jnp.int32(1), step[0] % levels)
    ordinal = jnp.arange(n_groups, dtype=jnp.int32)
    matches = cycle_order[:, None] == ordinal[None, :]
    position = jnp.sum(jnp.where(matches, ordinal[:, None], 0), axis=0)
    source_pos = (position - distance) % n_groups
    sources = jnp.sum(
        jnp.where(source_pos[:, None] == ordinal[None, :], cycle_order[None, :], 0), axis=1
    )
    flattened = stepped.reshape(n_groups, -1)
    weight_tiles = jnp.full((n_groups,), weight, jnp.float32)
    received, received_w = (
        lax.all_to_all(
            flattened.astype(jnp.bfloat16), "gossip", split_axis=0, concat_axis=0, tiled=True
        ).astype(flattened.dtype),
        lax.all_to_all(
            weight_tiles.astype(jnp.bfloat16), "gossip", split_axis=0, concat_axis=0, tiled=True
        ).astype(weight_tiles.dtype),
    )
    outgoing = jnp.take(received, sources, axis=0)
    outgoing_w = jnp.take(received_w, sources, axis=0)
    arrived, arrived_w = (
        lax.all_to_all(
            outgoing.astype(jnp.bfloat16), "gossip", split_axis=0, concat_axis=0, tiled=True
        ).astype(outgoing.dtype),
        lax.all_to_all(
            outgoing_w.astype(jnp.bfloat16), "gossip", split_axis=0, concat_axis=0, tiled=True
        ).astype(outgoing_w.dtype),
    )
    partner = arrived.reshape(stepped.shape)
    new_params = 0.5 * stepped + 0.5 * partner
    new_weight = 0.5 * weight + 0.5 * arrived_w[0]
    return (grad_in[None], new_params[None], jnp.reshape(new_weight, (1,)))


def solution(mesh):
    placed = (
        P("gossip", "shard", None),
        P("gossip", "shard", None),
        P("gossip", "shard", None),
        P("gossip"),
        P(),
        P(),
    )
    return jax.shard_map(
        body,
        mesh=mesh,
        in_specs=placed,
        out_specs=(P("gossip", "shard", None), P("gossip", "shard", None), P("gossip")),
        check_vma=False,
    )
```

profile of v0, /device:TPU:8, one launch (start us, length us, event | category | flops | bytes accessed | tf_op | source)
XLA Modules:
  0.0 442.8 jit_solution(7423503846964349468)
XLA Ops:
  7.2 0.0 all-gather.2.cloned.1.call-start
  7.9 1.6 fusion.9
  9.5 0.0 all-gather.2.cloned.1.call-update
  9.5 0.0 all-reduce.3.cloned.1.call-start
  9.6 71.2 %all-gather.2.cloned.1.call-done = bf16[2048,1010]{1,0:T(8,128)(2,1)} async-done(((bf16[64,1010]{1,0:T(8,128)(2,1)}), bf16[2048,1010]{1,0:T(8,128)(2,1)}) %all-gather.2.cloned.1.call-update) | async-done | bytes 4136976 | tf_op jit(solution)/shard_map/all_gather | solution.py:21
  80.8 0.0 copy-start.1
  80.8 5.5 %fusion.2 = bf16[432,1010]{1,0:T(8,128)(2,1)S(1)} fusion(bf16[2048,1010]{1,0:T(8,128)(2,1)} %all-gather.2.cloned.1.call-done, bf16[432,2020]{1,0:T(8,128)(2,1)} %bitcast.53, bf16[1,432,1010]{2,1,0:T(8,128)(2,1)} %param.7), kind=kOutput, calls=%fused_computation.7 | convolution fusion | flops 1791530240 | bytes 7627520 | tf_op jit(solution)/shard_map/dot_general | solution.py:22
  86.3 0.0 copy-done.1
  86.3 4.4 convolution_convert_fusion
  90.6 0.0 copy-start.2
  90.6 0.0 copy-start
  90.6 0.0 all-reduce.3.cloned.1.call-update
  90.7 0.6 broadcast_in_dim.56
  91.3 9.1 %all-to-all-start.2 = ((bf16[16,1,1]{2,1,0:T(2,128)(2,1)}), bf16[16,1,1]{2,1,0:T(2,128)(2,1)S(1)}, u32[]{:S(2)}, u32[]{:S(2)}) async-start(bf16[16,1,1]{2,1,0:T(2,128)(2,1)} %broadcast_in_dim.56), calls=%async_computation.2 | async-start | bytes 16384 | tf_op jit(solution)/shard_map/all_to_all | solution.py:51
  101.0 0.0 copy-done.2
  101.0 0.1 select_reduce_fusion.1
  101.2 0.2 select_reduce_fusion
  101.4 6.1 %all-to-all-done.2 = bf16[16,1,1]{2,1,0:T(2,128)(2,1)S(1)} async-done(((bf16[16,1,1]{2,1,0:T(2,128)(2,1)}), bf16[16,1,1]{2,1,0:T(2,128)(2,1)S(1)}, u32[]{:S(2)}, u32[]{:S(2)}) %all-to-all-start.2) | async-done | bytes 64 | tf_op jit(solution)/shard_map/all_to_all | solution.py:51
  107.5 0.2 convert_reduce_fusion.1
  107.7 0.7 gather_fusion.1
  108.4 0.7 copy.20
  109.1 4.7 %all-to-all-start.3 = ((bf16[16,1,1]{2,1,0:T(2,128)(2,1)}), bf16[16,1,1]{2,1,0:T(2,128)(2,1)S(1)}, u32[]{:S(2)}, u32[]{:S(2)}) async-start(bf16[16,1,1]{2,1,0:T(2,128)(2,1)} %copy.20), calls=%async_computation.3 | async-start | bytes 16384 | tf_op jit(solution)/shard_map/all_to_all | solution.py:61
  113.8 7.3 %all-to-all-done.3 = bf16[16,1,1]{2,1,0:T(2,128)(2,1)S(1)} async-done(((bf16[16,1,1]{2,1,0:T(2,128)(2,1)}), bf16[16,1,1]{2,1,0:T(2,128)(2,1)S(1)}, u32[]{:S(2)}, u32[]{:S(2)}) %all-to-all-start.3) | async-done | bytes 64 | tf_op jit(solution)/shard_map/all_to_all | solution.py:61
  121.0 0.5 slice.16
  122.2 272.0 %all-reduce.3.cloned.1.call-done = bf16[2048,1010]{1,0:T(8,128)(2,1)} async-done(((bf16[2048,1010]{1,0:T(8,128)(2,1)}), bf16[2048,1010]{1,0:T(8,128)(2,1)}) %all-reduce.3.cloned.1.call-update) | async-done | bytes 4136976 | tf_op jit(solution)/shard_map/psum | solution.py:31
  394.2 0.0 copy-done
  394.2 0.9 fusion.10
  395.2 0.2 convert_element_type.100
  395.4 0.5 broadcast.159
  395.9 1.4 reduce.4
  397.4 0.8 reshape.158
  398.2 10.3 %all-to-all-start = ((bf16[16,2,2020]{2,1,0:T(2,128)(2,1)}), bf16[16,2,2020]{2,1,0:T(2,128)(2,1)S(1)}, u32[]{:S(2)}, u32[]{:S(2)}) async-start(bf16[16,2,2020]{2,1,0:T(2,128)(2,1)} %reshape.158), calls=%async_computation | async-start | bytes 262144 | tf_op jit(solution)/shard_map/all_to_all | solution.py:48
  408.6 4.2 fusion.16
  412.8 4.2 all-to-all-done
  417.0 0.2 reshape.159
  417.2 0.2 copy.22
  417.3 0.6 gather_fusion
  418.0 0.1 fusion.8
  418.0 0.7 reduce.5
  418.7 0.8 reshape.160
  419.6 4.1 all-to-all-start.1
  423.6 1.3 fusion
  424.9 7.2 %all-to-all-done.1 = bf16[16,2,2020]{2,1,0:T(2,128)(2,1)S(1)} async-done(((bf16[16,2,2020]{2,1,0:T(2,128)(2,1)}), bf16[16,2,2020]{2,1,0:T(2,128)(2,1)S(1)}, u32[]{:S(2)}, u32[]{:S(2)}) %all-to-all-start.1) | async-done | bytes 129312 | tf_op jit(solution)/shard_map/all_to_all | solution.py:58
  432.1 0.2 reshape.161
  432.3 0.7 convert_reduce_fusion
  433.0 0.1 reshape.137
  433.1 1.7 multiply_bitcast_fusion
  (5 shorter events, 0.0 us)
Async XLA Ops:
  7.2 73.6 %all-gather.2.cloned.1.call-start = ((), (), s32[]{:S(2)}) async-start(), calls=%async_computation.4 | async-start | bytes 4325376 | tf_op jit(solution)/shard_map/all_gather | solution.py:21
  9.5 384.7 %all-reduce.3.cloned.1.call-start = ((), (), s32[]{:S(2)}) async-start(), calls=%async_computation.5 | async-start | bytes 8388608 | tf_op jit(solution)/shard_map/psum | solution.py:31
  80.8 5.5 %copy-start.1 = (bf16[1,432,2020]{2,1,0:T(8,128)(2,1)S(1)}, bf16[1,432,2020]{2,1,0:T(8,128)(2,1)}, u32[]{:S(2)}) copy-start(bf16[1,432,2020]{2,1,0:T(8,128)(2,1)} %param.6) | copy-start | bytes 5235844
  90.6 10.4 %copy-start.2 = (s32[16]{0:T(128)S(1)}, s32[16]{0:T(128)}, u32[]{:S(2)}) copy-start(s32[16]{0:T(128)} %param.11) | copy-start | bytes 196
  90.6 303.6 %copy-start = (f32[1,64,1010]{2,1,0:T(8,128)S(1)}, f32[1,64,1010]{2,1,0:T(8,128)}, u32[]{:S(2)}) copy-start(f32[1,64,1010]{2,1,0:T(8,128)} %param.8) | copy-start | bytes 775684
  91.3 16.2 %all-to-all-start.2 = ((bf16[16,1,1]{2,1,0:T(2,128)(2,1)}), bf16[16,1,1]{2,1,0:T(2,128)(2,1)S(1)}, u32[]{:S(2)}, u32[]{:S(2)}) async-start(bf16[16,1,1]{2,1,0:T(2,128)(2,1)} %broadcast_in_dim.56), calls=%async_computation.2 | async-start | bytes 16384 | tf_op jit(solution)/shard_map/all_to_all | solution.py:51
  109.1 12.0 %all-to-all-start.3 = ((bf16[16,1,1]{2,1,0:T(2,128)(2,1)}), bf16[16,1,1]{2,1,0:T(2,128)(2,1)S(1)}, u32[]{:S(2)}, u32[]{:S(2)}) async-start(bf16[16,1,1]{2,1,0:T(2,128)(2,1)} %copy.20), calls=%async_computation.3 | async-start | bytes 16384 | tf_op jit(solution)/shard_map/all_to_all | solution.py:61
  398.2 18.8 %all-to-all-start = ((bf16[16,2,2020]{2,1,0:T(2,128)(2,1)}), bf16[16,2,2020]{2,1,0:T(2,128)(2,1)S(1)}, u32[]{:S(2)}, u32[]{:S(2)}) async-start(bf16[16,2,2020]{2,1,0:T(2,128)(2,1)} %reshape.158), calls=%async_computation | async-start | bytes 262144 | tf_op jit(solution)/shard_map/all_to_all | solution.py:48
  419.6 12.5 %all-to-all-start.1 = ((bf16[16,2,2020]{2,1,0:T(2,128)(2,1)}), bf16[16,2,2020]{2,1,0:T(2,128)(2,1)S(1)}, u32[]{:S(2)}, u32[]{:S(2)}) async-start(bf16[16,2,2020]{2,1,0:T(2,128)(2,1)} %reshape.160), calls=%async_computation.1 | async-start | bytes 262144 | tf_op jit(solution)/shard_map/all_to_all | solution.py:58
Sparse Core Ops, SparseCore 0:
  11.7 69.0 all-gather.1
  90.8 303.4 all-reduce.2
where the time goes:
time: 443 us
  waiting for transfers between devices  368 us (83%)
  starting transfers between devices  28.3 us (6%)
  between operations  17.3 us (4%)
  matrix products  14.1 us (3%)
  other arithmetic  7.69 us (2%)
  local copies, waits for them, and re-layouts  7.46 us (2%)
    psum x1, waiting for transfers between devices, body(): lax.psum(local_grad.astype(jnp.bfloat16), 'shard').astype(jnp.float32)  272 us
    all_gather x1, waiting for transfers between devices, body(): gathered = lax.all_gather(debiased, 'shard', axis=0, tiled=True)  71.2 us
    all_to_all x1, starting transfers between devices, body(): lax.all_to_all(flattened.astype(jnp.bfloat16), 'gossip', split_axis=0, co...  10.3 us
    all_to_all x1, starting transfers between devices, body(): lax.all_to_all(weight_tiles.astype(jnp.bfloat16), 'gossip', split_axis=0,...  9.08 us
  transfers between devices with their start and end apart: 6, of which 6 were waited for; matrix products, arithmetic and copies ran while one was open for 2% of the time, Pallas kernels for 0%

commit v1 on v0

--- a/solution.py
+++ b/solution.py
@@ -18,7 +18,8 @@
     x_padded = jnp.pad(x_rows, ((0, 0), (0, padded_width - in_width)))
     debiased = (own_shard / weight).astype(jnp.bfloat16)
     contract_cols = (((1,), (1,)), ((), ()))
-    gathered = lax.all_gather(debiased, "shard", axis=0, tiled=True)
+    stack = jnp.stack([debiased] * lax.axis_size("shard"))
+    gathered = jnp.concatenate(lax.all_to_all(stack, "shard", 0, 0), axis=0)
     pre_act = jnp.dot(x_padded, gathered, preferred_element_type=jnp.float32)
     sigmoid_pre = jax.nn.sigmoid(pre_act)
     d_pre = (

time: 443 us -> 479 us (1.081)
  blocking collectives: 0 us -> 89.2 us
  waiting for transfers between devices: 368 us -> 296 us
  starting transfers between devices: 28.3 us -> 48.2 us
    all_to_all x0 -> x1, blocking collectives: none -> 89.2 us  [body(): gathered = jnp.concatenate(lax.all_to_all(stack, 'shard', 0, 0), axis=0)]
    all_gather x1 -> x0, waiting for transfers between devices: 71.2 us -> none  [body(): gathered = lax.all_gather(debiased, 'shard', axis=0, tiled=True)]
    all_to_all x1, starting transfers between devices: 9.08 us -> 29.1 us  [body(): lax.all_to_all(weight_tiles.astype(jnp.bfloat16), 'gossip', split_axis=0,...]
  transfers between devices with their start and end apart: 6 -> 5, of which waited for: 6 -> 5; matrix products, arithmetic and copies ran while one was open for 2% -> 2% of each run, Pallas kernels for 0% -> 0%
where the time goes in v1:
time: 479 us; the launch traced here: 478 us
  waiting for transfers between devices  296 us (62%)
  blocking collectives  89.2 us (19%)
  starting transfers between devices  48.2 us (10%)
  between operations  17.3 us (4%)
  matrix products  11.1 us (2%)
  local copies, waits for them, and re-layouts  9.91 us (2%)
  other arithmetic  7 us (1%)
    psum x1, waiting for transfers between devices, body(): lax.psum(local_grad.astype(jnp.bfloat16), 'shard').astype(jnp.float32)  271 us
    all_to_all x1, blocking collectives, body(): gathered = jnp.concatenate(lax.all_to_all(stack, 'shard', 0, 0), axis=0)  89.2 us
    all_to_all x1, starting transfers between devices, body(): lax.all_to_all(weight_tiles.astype(jnp.bfloat16), 'gossip', split_axis=0,...  29.1 us
    all_to_all x1, starting transfers between devices, body(): lax.all_to_all(flattened.astype(jnp.bfloat16), 'gossip', split_axis=0, co...  10.3 us
  transfers between devices with their start and end apart: 5, of which 5 were waited for; matrix products, arithmetic and copies ran while one was open for 2% of the time, Pallas kernels for 0%

profile of v1, /device:TPU:8, one launch (start us, length us, event | category | flops | bytes accessed | tf_op | source)
XLA Modules:
  0.0 478.3 jit_solution(15681595358421870643)
XLA Ops:
  7.2 0.0 all-reduce.3.cloned.1.call-start
  7.9 1.0 fusion.10
  8.8 0.5 stack.5
  9.4 0.0 copy-start.2
  9.4 0.0 copy-start.3
  9.4 89.2 %all_to_all.29 = bf16[32,64,1010]{2,1,0:T(8,128)(2,1)S(1)} all-to-all(bf16[32,64,1010]{2,1,0:T(8,128)(2,1)S(1)} %stack.5), channel_id=1, replica_groups=mesh['gossip'=16,'shard'=32] {'shard'}, dimensions={0} | all-to-all | bytes 8273920 | tf_op jit(solution)/shard_map/all_to_all | solution.py:22
  98.6 0.0 copy-start
  98.6 1.9 copy-done
  100.5 0.0 copy-done.2
  100.5 0.0 copy-done.3
  100.5 2.5 fusion.2
  103.0 4.4 convolution_convert_fusion
  107.4 0.0 all-reduce.3.cloned.1.call-update
  107.4 0.6 broadcast_in_dim.56
  108.0 29.1 %all-to-all-start.3 = ((bf16[16,1,1]{2,1,0:T(2,128)(2,1)}), bf16[16,1,1]{2,1,0:T(2,128)(2,1)S(1)}, u32[]{:S(2)}, u32[]{:S(2)}) async-start(bf16[16,1,1]{2,1,0:T(2,128)(2,1)} %broadcast_in_dim.56), calls=%async_computation.3 | async-start | bytes 16384 | tf_op jit(solution)/shard_map/all_to_all | solution.py:52
  137.8 0.0 copy-done.4
  137.8 0.1 select_reduce_fusion.1
  137.9 0.2 select_reduce_fusion
  138.1 6.1 %all-to-all-done.3 = bf16[16,1,1]{2,1,0:T(2,128)(2,1)S(1)} async-done(((bf16[16,1,1]{2,1,0:T(2,128)(2,1)}), bf16[16,1,1]{2,1,0:T(2,128)(2,1)S(1)}, u32[]{:S(2)}, u32[]{:S(2)}) %all-to-all-start.3) | async-done | bytes 64 | tf_op jit(solution)/shard_map/all_to_all | solution.py:52
  144.2 0.2 convert_reduce_fusion.1
  144.4 0.7 gather_fusion.1
  145.1 0.7 copy.20
  145.8 4.7 all-to-all-start.4
  150.5 7.2 %all-to-all-done.4 = bf16[16,1,1]{2,1,0:T(2,128)(2,1)S(1)} async-done(((bf16[16,1,1]{2,1,0:T(2,128)(2,1)}), bf16[16,1,1]{2,1,0:T(2,128)(2,1)S(1)}, u32[]{:S(2)}, u32[]{:S(2)}) %all-to-all-start.4) | async-done | bytes 64 | tf_op jit(solution)/shard_map/all_to_all | solution.py:62
  157.7 0.5 slice.16
  158.8 271.0 %all-reduce.3.cloned.1.call-done = bf16[2048,1010]{1,0:T(8,128)(2,1)} async-done(((bf16[2048,1010]{1,0:T(8,128)(2,1)}), bf16[2048,1010]{1,0:T(8,128)(2,1)}) %all-reduce.3.cloned.1.call-update) | async-done | bytes 4136976 | tf_op jit(solution)/shard_map/psum | solution.py:32
  429.8 0.0 copy-done.1
  429.8 0.9 fusion.9
  430.8 0.2 convert_element_type.101
  431.0 0.5 broadcast.161
  431.5 1.4 reduce.4
  432.9 0.8 reshape.163
  433.8 10.3 %all-to-all-start.1 = ((bf16[16,2,2020]{2,1,0:T(2,128)(2,1)}), bf16[16,2,2020]{2,1,0:T(2,128)(2,1)S(1)}, u32[]{:S(2)}, u32[]{:S(2)}) async-start(bf16[16,2,2020]{2,1,0:T(2,128)(2,1)} %reshape.163), calls=%async_computation.1 | async-start | bytes 262144 | tf_op jit(solution)/shard_map/all_to_all | solution.py:49
  444.1 4.2 fusion.16
  448.3 4.2 all-to-all-done.1
  452.5 0.2 reshape.164
  452.7 0.2 copy.22
  452.9 0.6 gather_fusion
  453.5 0.1 fusion.8
  453.6 0.7 reduce.5
  454.3 0.8 reshape.165
  455.1 4.1 all-to-all-start.2
  459.2 1.3 fusion
  460.5 7.2 %all-to-all-done.2 = bf16[16,2,2020]{2,1,0:T(2,128)(2,1)S(1)} async-done(((bf16[16,2,2020]{2,1,0:T(2,128)(2,1)}), bf16[16,2,2020]{2,1,0:T(2,128)(2,1)S(1)}, u32[]{:S(2)}, u32[]{:S(2)}) %all-to-all-start.2) | async-done | bytes 129312 | tf_op jit(solution)/shard_map/all_to_all | solution.py:59
  467.6 0.2 reshape.166
  467.8 0.7 convert_reduce_fusion
  468.6 0.1 reshape.142
  468.7 1.7 multiply_bitcast_fusion
  (7 shorter events, 0.0 us)
Async XLA Ops:
  7.2 422.7 %all-reduce.3.cloned.1.call-start = ((), (), s32[]{:S(2)}) async-start(), calls=%async_computation.5 | async-start | bytes 8388608 | tf_op jit(solution)/shard_map/psum | solution.py:32
  9.4 91.2 %copy-start.2 = (bf16[1,432,2020]{2,1,0:T(8,128)(2,1)S(1)}, bf16[1,432,2020]{2,1,0:T(8,128)(2,1)}, u32[]{:S(2)}) copy-start(bf16[1,432,2020]{2,1,0:T(8,128)(2,1)} %param.6) | copy-start | bytes 5235844
  9.4 91.2 %copy-start.3 = (bf16[1,432,1010]{2,1,0:T(8,128)(2,1)S(1)}, bf16[1,432,1010]{2,1,0:T(8,128)(2,1)}, u32[]{:S(2)}) copy-start(bf16[1,432,1010]{2,1,0:T(8,128)(2,1)} %param.7) | copy-start | bytes 2617924
  98.6 1.9 copy-start
  107.4 30.4 %copy-start.4 = (s32[16]{0:T(128)S(1)}, s32[16]{0:T(128)}, u32[]{:S(2)}) copy-start(s32[16]{0:T(128)} %param.11) | copy-start | bytes 196
  107.4 322.4 %copy-start.1 = (f32[1,64,1010]{2,1,0:T(8,128)S(1)}, f32[1,64,1010]{2,1,0:T(8,128)}, u32[]{:S(2)}) copy-start(f32[1,64,1010]{2,1,0:T(8,128)} %param.8) | copy-start | bytes 775684
  108.0 36.2 %all-to-all-start.3 = ((bf16[16,1,1]{2,1,0:T(2,128)(2,1)}), bf16[16,1,1]{2,1,0:T(2,128)(2,1)S(1)}, u32[]{:S(2)}, u32[]{:S(2)}) async-start(bf16[16,1,1]{2,1,0:T(2,128)(2,1)} %broadcast_in_dim.56), calls=%async_computation.3 | async-start | bytes 16384 | tf_op jit(solution)/shard_map/all_to_all | solution.py:52
  145.8 11.9 %all-to-all-start.4 = ((bf16[16,1,1]{2,1,0:T(2,128)(2,1)}), bf16[16,1,1]{2,1,0:T(2,128)(2,1)S(1)}, u32[]{:S(2)}, u32[]{:S(2)}) async-start(bf16[16,1,1]{2,1,0:T(2,128)(2,1)} %copy.20), calls=%async_computation.4 | async-start | bytes 16384 | tf_op jit(solution)/shard_map/all_to_all | solution.py:62
  433.8 18.8 %all-to-all-start.1 = ((bf16[16,2,2020]{2,1,0:T(2,128)(2,1)}), bf16[16,2,2020]{2,1,0:T(2,128)(2,1)S(1)}, u32[]{:S(2)}, u32[]{:S(2)}) async-start(bf16[16,2,2020]{2,1,0:T(2,128)(2,1)} %reshape.163), calls=%async_computation.1 | async-start | bytes 262144 | tf_op jit(solution)/shard_map/all_to_all | solution.py:49
  455.1 12.5 %all-to-all-start.2 = ((bf16[16,2,2020]{2,1,0:T(2,128)(2,1)}), bf16[16,2,2020]{2,1,0:T(2,128)(2,1)S(1)}, u32[]{:S(2)}, u32[]{:S(2)}) async-start(bf16[16,2,2020]{2,1,0:T(2,128)(2,1)} %reshape.165), calls=%async_computation.2 | async-start | bytes 262144 | tf_op jit(solution)/shard_map/all_to_all | solution.py:59
Sparse Core Ops, SparseCore 0:
  107.5 322.2 all-reduce.2
